TPU v7x, 256 devices: a whole 4x4x8 slice. The times are simulated.
256 devices in a mesh: grp: 16 (over y, z_hi, core), dev: 16 (over z_lo, x).
Axes of the slice: x: 4, y: 4, z: 8 (z_hi: 2, z_lo: 4; z = z_hi * 4 + z_lo), core: 2. Of those that a mesh axis runs over, the one named last changes fastest.
Arguments:
- panels: bfloat16 [256, 1536, 512], P(('grp', 'dev')), may hold values from -0.19921875 to 0.19921875
- panel_owner: int32 [16, 3], replicated, may hold values from 0 to 15, as said below
- interface_cols: bfloat16 [1536, 65536], P(None, ('grp', 'dev')), may hold values from -6 to 6
- border: bfloat16 [16384, 1536], P('grp', 'dev'), may hold values from -0.15625 to 0.15625
- block_rows: int32 [16, 8], replicated, may hold values from 0 to 31, as said below
- pattern: int32 [32, 32], P('grp', 'dev'), may hold values 0 or 1
- block_x: bfloat16 [4096, 256], P('dev'), may hold values from -0.09375 to 0.09375
Outputs:
- schur: bfloat16 [4096, 4096], P('grp', 'dev')
- product: float32 [4096, 256], P('grp')
Inputs may be any that keep to these rules, and one draw needn't show every extreme that they name: `panel_owner`: in each row the values are distinct. `block_rows`: in each row the values are distinct; for each subdomain the block rows with the same value of block // 2 (their owner group) come exactly 2 at a time; in every draw some owner group receives 2 block rows from every subdomain.
All inputs are finite; a program needn't handle non-finite values. No bound on the sum of `pattern` on one device may be relied on, other than what follows from the above.
Results may differ from a plain program's by a relative error of at most 0.017.
Values may be sent and summed in bfloat16 or wider, within the bound.
No kernel may reach another device: no remote copies, remote signals or barrier semaphores. Data moves between devices by JAX's collectives and lax.ppermute only.
A program may use at most 64 MiB of HBM per device.

v0:
```python
import jax
import jax.numpy as jnp
from jax import lax
from jax.sharding import PartitionSpec as P


def from_root(value, axis, source):
    kept = jnp.where(lax.axis_index(axis) == source, value, 0).astype(value.dtype)
    return lax.psum(kept, axis)


def local(panels, panel_owner, interface_cols, border, block_rows, pattern, block_x):
    group = lax.axis_index("grp")
    owners = lax.dynamic_slice_in_dim(panel_owner, group, 1, 0)[0]
    stored = panels[0]
    width = stored.shape[1]
    count_panels = stored.shape[0] // width
    columns = interface_cols.shape[1]
    lower = lax.broadcasted_iota(jnp.int32, (width, width), 0) > lax.broadcasted_iota(
        jnp.int32, (width, width), 1
    )
    unit = jnp.eye(width, dtype=jnp.bfloat16)
    remain = [
        interface_cols[step * width : (step + 1) * width].astype(jnp.float32)
        for step in range(count_panels)
    ]
    solved = []
    for step in range(count_panels):
        received = from_root(stored[step * width :], "dev", owners[step])
        inverse = jnp.where(lower, received[:width], jnp.zeros((), jnp.bfloat16)) + unit
        current = jnp.dot(
            inverse, remain[step].astype(jnp.bfloat16), preferred_element_type=jnp.float32
        ).astype(jnp.bfloat16)
        solved.append(current)
        if step + 1 < count_panels:
            below = jnp.dot(received[width:], current, preferred_element_type=jnp.float32)
            for later in range(step + 1, count_panels):
                offset = (later - step - 1) * width
                remain[later] = remain[later] - below[offset : offset + width]
    answer = jnp.concatenate(solved, axis=0)
    tile = jnp.dot(
        lax.all_gather(border, "dev", axis=1, tiled=True),
        answer,
        preferred_element_type=jnp.float32,
    )
    owned = pattern.shape[0]
    col_blocks = pattern.shape[1]
    block_size = columns // col_blocks
    per_group = block_rows.shape[1]
    tile_flat = tile.reshape(per_group, block_size * columns)
    my_list = lax.dynamic_slice_in_dim(block_rows, group, 1, 0)[0]
    targets = lax.broadcasted_iota(jnp.int32, (owned * lax.axis_size("grp"), 1), 0)
    onehot = (targets == my_list[None, :]).astype(jnp.float32)
    own_rows = lax.psum_scatter(
        jnp.dot(
            onehot, tile_flat, precision=lax.Precision.HIGHEST, preferred_element_type=jnp.float32
        ),
        "grp",
        scatter_dimension=0,
        tiled=True,
    )
    masked = (
        own_rows.reshape(owned, block_size, col_blocks, block_size)
        * pattern.astype(jnp.float32)[:, None, :, None]
    )
    schur = masked.reshape(owned * block_size, columns).astype(jnp.bfloat16)
    partial_sum = jnp.dot(schur, block_x, preferred_element_type=jnp.float32)
    product = lax.psum(partial_sum.astype(jnp.bfloat16), "dev").astype(jnp.float32)
    return (schur, product)


def solution(mesh):
    return jax.shard_map(
        local,
        mesh=mesh,
        in_specs=(
            P(("grp", "dev"), None, None),
            P(),
            P(None, ("grp", "dev")),
            P("grp", "dev"),
            P(),
            P("grp", "dev"),
            P("dev", None),
        ),
        out_specs=(P("grp", "dev"), P("grp", None)),
        check_vma=False,
    )
```

profile of v0, /device:TPU:8, one launch (start us, length us, event | category | flops | bytes accessed | tf_op | source)
XLA Modules:
  0.0 684.9 jit_solution(15940117969931973138)
XLA Ops:
  7.2 0.8 constant_dynamic-slice_fusion.1
  8.0 0.5 fusion.41
  9.8 1.3 select_bitcast_fusion
  11.1 0.7 copy-done.1
  11.8 1.1 select_bitcast_fusion.1
  13.5 0.9 select_bitcast_fusion.2
  14.5 0.7 all-gather.2.cloned.1.call-update
  15.4 175.8 %all-reduce.10.cloned.1.call-done = (bf16[1024,512]{1,0:T(8,128)(2,1)}, bf16[1536,512]{1,0:T(8,128)(2,1)}, bf16[512,512]{1,0:T(8,128)(2,1)}) async-done(((bf16[1024,512]{1,0:T(8,128)(2,1)}, bf16[1536,512]{1,0:T(8,128)(2,1)}, bf16[512,512]{1,0:T(8,128)(2,1)}), (bf16[1024,512]{1,0:T(8,128)(2,1)}, bf16[1536,512]{1,0:T(8,128)(2,1)}, bf16[512,512]{1,0:T(8,128)(2,1)})) %all-reduce.10.cloned.1.call-update) | async-done | bytes 3145744 | tf_op jit(solution)/shard_map/psum | solution.py:9
  191.2 1.5 convolution_convert_fusion.2
  192.8 0.4 fusion.1
  193.2 0.8 copy-done.6
  194.0 0.3 convolution_convert_fusion.1
  194.3 2.5 convolution_convert_fusion
  196.8 78.6 %all-gather.2.cloned.1.call-done = bf16[1024,1536]{0,1:T(8,128)(2,1)} async-done(((bf16[1024,96]{0,1:T(8,128)(2,1)}), bf16[1024,1536]{0,1:T(8,128)(2,1)}) %all-gather.2.cloned.1.call-update) | async-done | bytes 3145744 | tf_op jit(solution)/shard_map/all_gather | solution.py:42
  275.4 3.0 convolution_bitcast_fusion
  278.4 0.3 copy.10
  278.9 3.7 fusion.35
  282.7 0.6 copy-done.5
  283.4 0.6 dynamic-slice
  284.6 227.1 %all-reduce.8.cloned.1.call-done = f32[32,32768]{1,0:T(8,128)} async-done(((f32[32,32768]{1,0:T(8,128)}), f32[32,32768]{1,0:T(8,128)}) %all-reduce.8.cloned.1.call-update) | async-done | bytes 4194320
  511.7 1.3 constant_dynamic-slice_fusion
  513.5 0.8 convolution_convert_fusion.3
  514.4 162.4 %all-reduce.6.cloned.1.call-done = bf16[256,256]{1,0:T(8,128)(2,1)} async-done(((bf16[256,256]{1,0:T(8,128)(2,1)}), bf16[256,256]{1,0:T(8,128)(2,1)}) %all-reduce.6.cloned.1.call-update) | async-done | bytes 131088 | tf_op jit(solution)/shard_map/psum | solution.py:68
  676.7 1.6 convert_element_type.60
  (28 shorter events, 1.1 us)
Async XLA Ops:
  7.2 506.3 %copy-start = (bf16[256,256]{1,0:T(8,128)(2,1)S(1)}, bf16[256,256]{1,0:T(8,128)(2,1)}, u32[]{:S(2)}) copy-start(bf16[256,256]{1,0:T(8,128)(2,1)} %param.13) | copy-start | bytes 393220
  7.2 184.0 %all-reduce.10.cloned.1.call-start = ((), (), s32[]{:S(2)}) async-start(), calls=%async_computation.3 | async-start | bytes 6291456 | tf_op jit(solution)/shard_map/psum | solution.py:9
  9.8 2.0 copy-start.1
  14.4 0.8 copy-start.4
  14.4 176.8 %copy-start.7 = (bf16[1536,256]{1,0:T(8,128)(2,1)S(1)}, bf16[1536,256]{1,0:T(8,128)(2,1)}, u32[]{:S(2)}) copy-start(bf16[1536,256]{1,0:T(8,128)(2,1)} %param.9) | copy-start | bytes 2359300
  14.4 261.0 %all-gather.2.cloned.1.call-start = ((), (), s32[]{:S(2)}) async-start(), calls=%async_computation | async-start | bytes 3342336 | tf_op jit(solution)/shard_map/all_gather | solution.py:42
  15.2 496.5 %all-reduce.8.cloned.1.call-start = ((), (), s32[]{:S(2)}) async-start(), calls=%async_computation.2 | async-start | bytes 8388608
  191.2 1.6 copy-start.2
  192.8 1.2 copy-start.6
  282.7 0.7 copy-start.5
  282.7 0.7 copy-start.8
  282.7 394.0 %all-reduce.6.cloned.1.call-start = ((), (), s32[]{:S(2)}) async-start(), calls=%async_computation.1 | async-start | bytes 262144 | tf_op jit(solution)/shard_map/psum | solution.py:68
  513.5 164.9 %copy-start.3 = (bf16[256,256]{1,0:T(8,128)(2,1)}, bf16[256,256]{1,0:T(8,128)(2,1)S(1)}, u32[]{:S(2)}) copy-start(bf16[256,256]{1,0:T(8,128)(2,1)S(1)} %fusion.28) | copy-start | bytes 393220
Sparse Core Ops, SparseCore 0:
  14.6 176.6 all-reduce.9
  193.0 82.3 all-gather.1
  282.8 228.8 all-reduce.7
  514.8 161.9 all-reduce.5
where the time goes:
time: 685 us
  waiting for transfers between devices  645 us (94%)
  between operations  16.5 us (2%)
  matrix products  12.3 us (2%)
    unnamed x5, waiting for transfers between devices  228 us
    psum x1, waiting for transfers between devices, from_root(): return lax.psum(kept, axis)  176 us
    psum x1, waiting for transfers between devices, local(): lax.psum(partial_sum.astype(jnp.bfloat16), 'dev').astype(jnp.float32)  162 us
    all_gather x1, waiting for transfers between devices, local(): lax.all_gather(border, 'dev', axis=1, tiled=True)  78.6 us
  transfers between devices with their start and end apart: 4, of which 4 were waited for; matrix products, arithmetic and copies ran while one was open for 1% of the time, Pallas kernels for 0%

commit v1 on v0

--- a/solution.py
+++ b/solution.py
@@ -6,7 +6,7 @@
 
 def from_root(value, axis, source):
     kept = jnp.where(lax.axis_index(axis) == source, value, 0).astype(value.dtype)
-    return lax.psum(kept, axis)
+    return jnp.sum(lax.all_gather(kept, axis), axis=0)
 
 
 def local(panels, panel_owner, interface_cols, border, block_rows, pattern, block_x):

time: 685 us -> 1070 us (1.56)
  waiting for transfers between devices: 645 us -> 997 us
  other arithmetic: 4.89 us -> 32.8 us
    all_gather x0 -> x3, waiting for transfers between devices: none -> 542 us  [from_root(): return jnp.sum(lax.all_gather(kept, axis), axis=0)]
    psum x1 -> x0, waiting for transfers between devices: 176 us -> none  [from_root(): return lax.psum(kept, axis)]
    reduce_sum x0 -> x3, other arithmetic: none -> 27 us  [from_root(): return jnp.sum(lax.all_gather(kept, axis), axis=0)]
    all_gather x1, waiting for transfers between devices: 78.6 us -> 64.7 us  [local(): lax.all_gather(border, 'dev', axis=1, tiled=True)]
    unnamed x5 -> x7, waiting for transfers between devices: 228 us -> 228 us
  transfers between devices with their start and end apart: 4 -> 6, of which waited for: 4 -> 6; matrix products, arithmetic and copies ran while one was open for 1% -> 3% of each run, Pallas kernels for 0% -> 0%
where the time goes in v1:
time: 1070 us; the launch traced here: 1060 us
  waiting for transfers between devices  997 us (93%)
  other arithmetic  32.8 us (3%)
  between operations  16.8 us (2%)
  matrix products  12.3 us (1%)
    all_gather x3, waiting for transfers between devices, from_root(): return jnp.sum(lax.all_gather(kept, axis), axis=0)  542 us
    unnamed x7, waiting for transfers between devices  228 us
    psum x1, waiting for transfers between devices, local(): lax.psum(partial_sum.astype(jnp.bfloat16), 'dev').astype(jnp.float32)  162 us
    all_gather x1, waiting for transfers between devices, local(): lax.all_gather(border, 'dev', axis=1, tiled=True)  64.7 us
    reduce_sum x3, other arithmetic, from_root(): return jnp.sum(lax.all_gather(kept, axis), axis=0)  27 us
  transfers between devices with their start and end apart: 6, of which 6 were waited for; matrix products, arithmetic and copies ran while one was open for 3% of the time, Pallas kernels for 0%

profile of v1, /device:TPU:8, one launch (start us, length us, event | category | flops | bytes accessed | tf_op | source)
XLA Modules:
  0.0 1064.7 jit_solution(9666441820864015976)
XLA Ops:
  7.2 0.9 constant_dynamic-slice_fusion.1
  9.3 1.9 slice_select_fusion.1
  11.9 1.1 slice_select_fusion
  13.5 1.3 broadcast_select_fusion
  15.7 100.9 %all-gather.9.cloned.1.call-done = bf16[16,512,512]{2,1,0:T(8,128)(2,1)} async-done(((bf16[1,512,512]{2,1,0:T(8,128)(2,1)}), bf16[16,512,512]{2,1,0:T(8,128)(2,1)}) %all-gather.9.cloned.1.call-update) | async-done | bytes 8388624 | tf_op jit(solution)/shard_map/all_gather | solution.py:9
  116.6 4.8 reduce_sum.38
  121.4 180.4 %all-gather.7.cloned.1.call-done = bf16[16,1024,512]{2,1,0:T(8,128)(2,1)} async-done(((bf16[1,1024,512]{2,1,0:T(8,128)(2,1)}), bf16[16,1024,512]{2,1,0:T(8,128)(2,1)}) %all-gather.7.cloned.1.call-update) | async-done | bytes 16777232 | tf_op jit(solution)/shard_map/all_gather | solution.py:9
  301.8 8.9 reduce_sum.37
  310.7 260.6 %all-gather.5.cloned.1.call-done = bf16[16,1536,512]{2,1,0:T(8,128)(2,1)} async-done(((bf16[1,1536,512]{2,1,0:T(8,128)(2,1)}), bf16[16,1536,512]{2,1,0:T(8,128)(2,1)}) %all-gather.5.cloned.1.call-update) | async-done | bytes 25165840 | tf_op jit(solution)/shard_map/all_gather | solution.py:9
  571.3 13.2 %reduce_sum.36 = bf16[1536,512]{1,0:T(8,128)(2,1)S(1)} reduce(bf16[16,1536,512]{2,1,0:T(8,128)(2,1)} %all-gather.5.cloned.1.call-done, bf16[]{:T(256)} %constant.17.clone.1), dimensions={0}, to_apply=%region_0.1 | reduce | flops 11796480 | bytes 26738690 | tf_op jit(solution)/shard_map/reduce_sum | solution.py:9
  584.5 1.2 convolution_convert_fusion.2
  586.2 1.0 copy-done.2
  587.2 1.3 convolution_convert_fusion.1
  588.5 1.8 convolution_convert_fusion
  590.3 64.7 %all-gather.11.cloned.1.call-done = bf16[1024,1536]{0,1:T(8,128)(2,1)} async-done(((bf16[1024,96]{0,1:T(8,128)(2,1)}), bf16[1024,1536]{0,1:T(8,128)(2,1)}) %all-gather.11.cloned.1.call-update) | async-done | bytes 3145744 | tf_op jit(solution)/shard_map/all_gather | solution.py:42
  655.0 2.9 convolution_bitcast_fusion
  658.4 3.8 fusion.35
  662.3 0.6 copy-done.5
  662.9 0.6 dynamic-slice
  664.1 227.1 %all-reduce.6.cloned.1.call-done = f32[32,32768]{1,0:T(8,128)} async-done(((f32[32,32768]{1,0:T(8,128)}), f32[32,32768]{1,0:T(8,128)}) %all-reduce.6.cloned.1.call-update) | async-done | bytes 4194320
  891.2 1.3 constant_dynamic-slice_fusion
  893.0 0.8 convolution_convert_fusion.3
  893.8 162.4 %all-reduce.4.cloned.1.call-done = bf16[256,256]{1,0:T(8,128)(2,1)} async-done(((bf16[256,256]{1,0:T(8,128)(2,1)}), bf16[256,256]{1,0:T(8,128)(2,1)}) %all-reduce.4.cloned.1.call-update) | async-done | bytes 131088 | tf_op jit(solution)/shard_map/psum | solution.py:68
  1056.2 1.6 convert_element_type.66
  (33 shorter events, 3.0 us)
Async XLA Ops:
  7.2 885.8 %copy-start = (bf16[256,256]{1,0:T(8,128)(2,1)S(1)}, bf16[256,256]{1,0:T(8,128)(2,1)}, u32[]{:S(2)}) copy-start(bf16[256,256]{1,0:T(8,128)(2,1)} %param.13) | copy-start | bytes 393220
  7.2 4.7 copy-start.1
  7.2 109.4 %all-gather.9.cloned.1.call-start = ((), (), s32[]{:S(2)}) async-start(), calls=%async_computation.2 | async-start | bytes 8912896 | tf_op jit(solution)/shard_map/all_gather | solution.py:9
  11.2 290.6 %all-gather.7.cloned.1.call-start = ((), (), s32[]{:S(2)}) async-start(), calls=%async_computation.1 | async-start | bytes 17825792 | tf_op jit(solution)/shard_map/all_gather | solution.py:9
  13.0 558.3 %all-gather.5.cloned.1.call-start = ((), (), s32[]{:S(2)}) async-start(), calls=%async_computation | async-start | bytes 26738688 | tf_op jit(solution)/shard_map/all_gather | solution.py:9
  14.8 0.7 copy-start.4
  14.9 640.1 %all-gather.11.cloned.1.call-start = ((), (), s32[]{:S(2)}) async-start(), calls=%async_computation.3 | async-start | bytes 3342336 | tf_op jit(solution)/shard_map/all_gather | solution.py:42
  15.4 875.8 %all-reduce.6.cloned.1.call-start = ((), (), s32[]{:S(2)}) async-start(), calls=%async_computation.5 | async-start | bytes 8388608
  586.2 1.0 copy-start.2
  662.2 0.7 copy-start.5
  662.2 0.7 copy-start.6
  662.2 394.0 %all-reduce.4.cloned.1.call-start = ((), (), s32[]{:S(2)}) async-start(), calls=%async_computation.4 | async-start | bytes 262144 | tf_op jit(solution)/shard_map/psum | solution.py:68
  893.0 164.9 %copy-start.3 = (bf16[256,256]{1,0:T(8,128)(2,1)}, bf16[256,256]{1,0:T(8,128)(2,1)S(1)}, u32[]{:S(2)}) copy-start(bf16[256,256]{1,0:T(8,128)(2,1)S(1)} %fusion.28) | copy-start | bytes 393220
Sparse Core Ops, SparseCore 0:
  11.3 105.2 all-gather.8
  118.4 183.3 all-gather.6
  303.6 267.6 all-gather.4
  572.9 82.0 all-gather.10
  662.3 228.8 all-reduce.5
  894.2 161.9 all-reduce.3

commit v2 on v0

--- a/solution.py
+++ b/solution.py
@@ -39,7 +39,9 @@
                 remain[later] = remain[later] - below[offset : offset + width]
     answer = jnp.concatenate(solved, axis=0)
     tile = jnp.dot(
-        lax.all_gather(border, "dev", axis=1, tiled=True),
+        jnp.concatenate(
+            lax.all_to_all(jnp.stack([border] * lax.axis_size("dev")), "dev", 0, 0), axis=1
+        ),
         answer,
         preferred_element_type=jnp.float32,
     )

time: 685 us -> 631 us (0.921)
  waiting for transfers between devices: 645 us -> 579 us
  starting transfers between devices: 0.16 us -> 8.77 us
    all_gather x1 -> x0, waiting for transfers between devices: 78.6 us -> none  [local(): lax.all_gather(border, 'dev', axis=1, tiled=True)]
    psum x1, waiting for transfers between devices: 176 us -> 189 us  [from_root(): return lax.psum(kept, axis)]
    all_to_all x0 -> x1, starting transfers between devices: none -> 8.64 us  [local(): lax.all_to_all(jnp.stack([border] * lax.axis_size('dev')), 'dev', 0, 0)]
    unnamed x5 -> x4, waiting for transfers between devices: 228 us -> 227 us
  transfers between devices with their start and end apart: 4 -> 4, of which waited for: 4 -> 3; matrix products, arithmetic and copies ran while one was open for 1% -> 1% of each run, Pallas kernels for 0% -> 0%
where the time goes in v2:
time: 631 us; the launch traced here: 630 us
  waiting for transfers between devices  579 us (92%)
  between operations  16.5 us (3%)
  matrix products  12.3 us (2%)
  local copies, waits for them, and re-layouts  8.79 us (1%)
  starting transfers between devices  8.77 us (1%)
    unnamed x4, waiting for transfers between devices  227 us
    psum x1, waiting for transfers between devices, from_root(): return lax.psum(kept, axis)  189 us
    psum x1, waiting for transfers between devices, local(): lax.psum(partial_sum.astype(jnp.bfloat16), 'dev').astype(jnp.float32)  163 us
  transfers between devices with their start and end apart: 4, of which 3 were waited for; matrix products, arithmetic and copies ran while one was open for 1% of the time, Pallas kernels for 0%

profile of v2, /device:TPU:8, one launch (start us, length us, event | category | flops | bytes accessed | tf_op | source)
XLA Modules:
  0.0 630.4 jit_solution(4260850122319694274)
XLA Ops:
  7.2 3.0 stack.2
  10.2 8.6 %all-to-all-start = ((bf16[16,1024,96]{1,2,0:T(8,128)(2,1)}), bf16[16,1024,96]{1,2,0:T(8,128)(2,1)}, u32[]{:S(2)}, u32[]{:S(2)}) async-start(bf16[16,1024,96]{1,2,0:T(8,128)(2,1)} %stack.2), calls=%async_computation | async-start | bytes 6291456 | tf_op jit(solution)/shard_map/all_to_all | solution.py:43
  19.0 0.6 fusion.41
  21.5 0.8 select_bitcast_fusion.2
  22.4 1.1 select_bitcast_fusion.1
  23.5 1.3 select_bitcast_fusion
  24.9 0.6 copy-done.4
  25.7 189.5 %all-reduce.10.cloned.1.call-done = (bf16[1024,512]{1,0:T(8,128)(2,1)}, bf16[1536,512]{1,0:T(8,128)(2,1)}, bf16[512,512]{1,0:T(8,128)(2,1)}) async-done(((bf16[1024,512]{1,0:T(8,128)(2,1)}, bf16[1536,512]{1,0:T(8,128)(2,1)}, bf16[512,512]{1,0:T(8,128)(2,1)}), (bf16[1024,512]{1,0:T(8,128)(2,1)}, bf16[1536,512]{1,0:T(8,128)(2,1)}, bf16[512,512]{1,0:T(8,128)(2,1)})) %all-reduce.10.cloned.1.call-update) | async-done | bytes 3145744 | tf_op jit(solution)/shard_map/psum | solution.py:9
  215.1 1.5 convolution_convert_fusion.2
  216.7 0.4 fusion.1
  217.1 0.8 copy-done.7
  217.9 0.3 convolution_convert_fusion.1
  218.3 2.5 convolution_convert_fusion
  220.8 3.0 convolution_bitcast_fusion
  223.7 0.3 copy.11
  224.3 3.7 fusion.35
  228.1 0.6 copy-done.6
  228.7 0.6 dynamic-slice
  229.9 227.2 %all-reduce.8.cloned.1.call-done = f32[32,32768]{1,0:T(8,128)} async-done(((f32[32,32768]{1,0:T(8,128)}), f32[32,32768]{1,0:T(8,128)}) %all-reduce.8.cloned.1.call-update) | async-done | bytes 4194320
  457.1 1.3 constant_dynamic-slice_fusion
  458.4 0.2 reshape.42
  458.9 0.8 convolution_convert_fusion.3
  459.7 162.5 %all-reduce.6.cloned.1.call-done = bf16[256,256]{1,0:T(8,128)(2,1)} async-done(((bf16[256,256]{1,0:T(8,128)(2,1)}), bf16[256,256]{1,0:T(8,128)(2,1)}) %all-reduce.6.cloned.1.call-update) | async-done | bytes 131088 | tf_op jit(solution)/shard_map/psum | solution.py:70
  622.3 1.6 convert_element_type.60
  (30 shorter events, 0.9 us)
Async XLA Ops:
  7.2 451.7 %copy-start = (bf16[256,256]{1,0:T(8,128)(2,1)S(1)}, bf16[256,256]{1,0:T(8,128)(2,1)}, u32[]{:S(2)}) copy-start(bf16[256,256]{1,0:T(8,128)(2,1)} %param.13) | copy-start | bytes 393220
  10.2 8.7 %copy-start.5 = (s32[16,3]{0,1:T(4,128)S(1)}, s32[16,3]{0,1:T(4,128)}, u32[]{:S(2)}) copy-start(s32[16,3]{0,1:T(4,128)} %param.8) | copy-start | bytes 580
  10.2 11.3 %copy-start.1 = (bf16[1,1536,512]{2,1,0:T(8,128)(2,1)S(1)}, bf16[1,1536,512]{2,1,0:T(8,128)(2,1)}, u32[]{:S(2)}) copy-start(bf16[1,1536,512]{2,1,0:T(8,128)(2,1)} %param.7) | copy-start | bytes 4718596
  10.2 210.5 %all-to-all-start = ((bf16[16,1024,96]{1,2,0:T(8,128)(2,1)}), bf16[16,1024,96]{1,2,0:T(8,128)(2,1)}, u32[]{:S(2)}, u32[]{:S(2)}) async-start(bf16[16,1024,96]{1,2,0:T(8,128)(2,1)} %stack.2), calls=%async_computation | async-start | bytes 6291456 | tf_op jit(solution)/shard_map/all_to_all | solution.py:43
  18.9 196.3 %all-reduce.10.cloned.1.call-start = ((), (), s32[]{:S(2)}) async-start(), calls=%async_computation.3 | async-start | bytes 6291456 | tf_op jit(solution)/shard_map/psum | solution.py:9
  24.8 0.7 copy-start.4
  24.8 190.3 %copy-start.8 = (bf16[1536,256]{1,0:T(8,128)(2,1)S(1)}, bf16[1536,256]{1,0:T(8,128)(2,1)}, u32[]{:S(2)}) copy-start(bf16[1536,256]{1,0:T(8,128)(2,1)} %param.9) | copy-start | bytes 2359300
  24.8 432.3 %all-reduce.8.cloned.1.call-start = ((), (), s32[]{:S(2)}) async-start(), calls=%async_computation.2 | async-start | bytes 8388608
  215.1 1.6 copy-start.2
  216.7 1.2 copy-start.7
  228.0 0.7 copy-start.6
  228.0 0.7 copy-start.9
  228.0 394.2 %all-reduce.6.cloned.1.call-start = ((), (), s32[]{:S(2)}) async-start(), calls=%async_computation.1 | async-start | bytes 262144 | tf_op jit(solution)/shard_map/psum | solution.py:70
  458.9 165.0 %copy-start.3 = (bf16[256,256]{1,0:T(8,128)(2,1)}, bf16[256,256]{1,0:T(8,128)(2,1)S(1)}, u32[]{:S(2)}) copy-start(bf16[256,256]{1,0:T(8,128)(2,1)S(1)} %fusion.28) | copy-start | bytes 393220
Sparse Core Ops, SparseCore 0:
  24.9 190.1 all-reduce.9
  228.2 228.9 all-reduce.7
  460.3 161.9 all-reduce.5

commit v3 on v0

--- a/solution.py
+++ b/solution.py
@@ -65,7 +65,9 @@
     )
     schur = masked.reshape(owned * block_size, columns).astype(jnp.bfloat16)
     partial_sum = jnp.dot(schur, block_x, preferred_element_type=jnp.float32)
-    product = lax.psum(partial_sum.astype(jnp.bfloat16), "dev").astype(jnp.float32)
+    product = jnp.sum(lax.all_gather(partial_sum.astype(jnp.bfloat16), "dev"), axis=0).astype(
+        jnp.float32
+    )
     return (schur, product)
 
 

time: 685 us -> 608 us (0.89)
  waiting for transfers between devices: 645 us -> 566 us
    psum x1 -> x0, waiting for transfers between devices: 162 us -> none  [local(): lax.psum(partial_sum.astype(jnp.bfloat16), 'dev').astype(jnp.float32)]
    all_gather x0 -> x1, waiting for transfers between devices: none -> 83.7 us  [local(): lax.all_gather(partial_sum.astype(jnp.bfloat16), 'dev')]
where the time goes in v3:
time: 608 us; the launch traced here: 607 us
  waiting for transfers between devices  566 us (93%)
  between operations  16.5 us (3%)
  matrix products  12.3 us (2%)
  local copies, waits for them, and re-layouts  6.48 us (1%)
    unnamed x5, waiting for transfers between devices  228 us
    psum x1, waiting for transfers between devices, from_root(): return lax.psum(kept, axis)  176 us
    all_gather x1, waiting for transfers between devices, local(): lax.all_gather(partial_sum.astype(jnp.bfloat16), 'dev')  83.7 us
    all_gather x1, waiting for transfers between devices, local(): lax.all_gather(border, 'dev', axis=1, tiled=True)  78.6 us
  transfers between devices with their start and end apart: 4, of which 4 were waited for; matrix products, arithmetic and copies ran while one was open for 1% of the time, Pallas kernels for 0%

profile of v3, /device:TPU:8, one launch (start us, length us, event | category | flops | bytes accessed | tf_op | source)
XLA Modules:
  0.0 607.2 jit_solution(14746926716882516615)
XLA Ops:
  7.2 0.8 constant_dynamic-slice_fusion.1
  8.0 0.5 fusion.41
  9.8 1.3 select_bitcast_fusion
  11.1 0.7 copy-done.1
  11.8 1.1 select_bitcast_fusion.1
  13.5 0.9 select_bitcast_fusion.2
  14.5 0.7 all-gather.4.cloned.1.call-update
  15.4 175.8 %all-reduce.7.cloned.1.call-done = (bf16[1024,512]{1,0:T(8,128)(2,1)}, bf16[1536,512]{1,0:T(8,128)(2,1)}, bf16[512,512]{1,0:T(8,128)(2,1)}) async-done(((bf16[1024,512]{1,0:T(8,128)(2,1)}, bf16[1536,512]{1,0:T(8,128)(2,1)}, bf16[512,512]{1,0:T(8,128)(2,1)}), (bf16[1024,512]{1,0:T(8,128)(2,1)}, bf16[1536,512]{1,0:T(8,128)(2,1)}, bf16[512,512]{1,0:T(8,128)(2,1)})) %all-reduce.7.cloned.1.call-update) | async-done | bytes 3145744 | tf_op jit(solution)/shard_map/psum | solution.py:9
  191.2 1.5 convolution_convert_fusion.2
  192.8 0.4 fusion.1
  193.2 0.8 copy-done.6
  194.0 0.3 convolution_convert_fusion.1
  194.3 2.5 convolution_convert_fusion
  196.8 78.6 %all-gather.4.cloned.1.call-done = bf16[1024,1536]{0,1:T(8,128)(2,1)} async-done(((bf16[1024,96]{0,1:T(8,128)(2,1)}), bf16[1024,1536]{0,1:T(8,128)(2,1)}) %all-gather.4.cloned.1.call-update) | async-done | bytes 3145744 | tf_op jit(solution)/shard_map/all_gather | solution.py:42
  275.4 3.0 convolution_bitcast_fusion
  278.9 3.7 fusion.35
  282.7 0.6 copy-done.5
  283.4 0.6 dynamic-slice
  284.6 227.1 %all-reduce.5.cloned.1.call-done = f32[32,32768]{1,0:T(8,128)} async-done(((f32[32,32768]{1,0:T(8,128)}), f32[32,32768]{1,0:T(8,128)}) %all-reduce.5.cloned.1.call-update) | async-done | bytes 4194320
  511.7 1.3 constant_dynamic-slice_fusion
  513.5 0.8 convolution_convert_fusion.3
  514.4 83.7 %all-gather.6.cloned.1.call-done = bf16[4096,256]{1,0:T(8,128)(2,1)} async-done(((bf16[256,256]{1,0:T(8,128)(2,1)}), bf16[4096,256]{1,0:T(8,128)(2,1)}) %all-gather.6.cloned.1.call-update) | async-done | bytes 2097168 | tf_op jit(solution)/shard_map/all_gather | solution.py:68
  598.0 1.9 reduce_sum.12
  599.9 0.7 convert_element_type.62
  (29 shorter events, 1.5 us)
Async XLA Ops:
  7.2 506.3 %copy-start = (bf16[256,256]{1,0:T(8,128)(2,1)S(1)}, bf16[256,256]{1,0:T(8,128)(2,1)}, u32[]{:S(2)}) copy-start(bf16[256,256]{1,0:T(8,128)(2,1)} %param.13) | copy-start | bytes 393220
  7.2 184.0 %all-reduce.7.cloned.1.call-start = ((), (), s32[]{:S(2)}) async-start(), calls=%async_computation.3 | async-start | bytes 6291456 | tf_op jit(solution)/shard_map/psum | solution.py:9
  9.8 2.0 copy-start.1
  14.4 0.8 copy-start.4
  14.4 176.8 %copy-start.7 = (bf16[1536,256]{1,0:T(8,128)(2,1)S(1)}, bf16[1536,256]{1,0:T(8,128)(2,1)}, u32[]{:S(2)}) copy-start(bf16[1536,256]{1,0:T(8,128)(2,1)} %param.9) | copy-start | bytes 2359300
  14.4 261.0 %all-gather.4.cloned.1.call-start = ((), (), s32[]{:S(2)}) async-start(), calls=%async_computation | async-start | bytes 3342336 | tf_op jit(solution)/shard_map/all_gather | solution.py:42
  15.2 496.5 %all-reduce.5.cloned.1.call-start = ((), (), s32[]{:S(2)}) async-start(), calls=%async_computation.2 | async-start | bytes 8388608
  191.2 1.6 copy-start.2
  192.8 1.2 copy-start.6
  282.7 0.7 copy-start.5
  282.7 0.7 copy-start.8
  282.7 315.3 %all-gather.6.cloned.1.call-start = ((), (), s32[]{:S(2)}) async-start(), calls=%async_computation.1 | async-start | bytes 2228224 | tf_op jit(solution)/shard_map/all_gather | solution.py:68
  513.5 87.2 %copy-start.3 = (bf16[256,256]{1,0:T(8,128)(2,1)}, bf16[256,256]{1,0:T(8,128)(2,1)S(1)}, u32[]{:S(2)}) copy-start(bf16[256,256]{1,0:T(8,128)(2,1)S(1)} %fusion.28) | copy-start | bytes 393220
Sparse Core Ops, SparseCore 0:
  14.6 176.6 all-reduce.6
  193.0 82.3 all-gather.3
  282.8 228.8 all-reduce.4
  514.5 83.5 all-gather.5
